TPU v7x, 128 devices: a whole 4x4x4 slice. The times are simulated.
128 devices in a mesh: ublk: 16 (over x, z), salt: 8 (over y, core).
Axes of the slice: x: 4, y: 4, z: 4, core: 2. Of those that a mesh axis runs over, the one named last changes fastest.
Arguments:
- user_factors: bfloat16 [16, 8192, 256], P('ublk', 'salt')
- tile_users: int32 [16, 8, 4096], P('ublk', 'salt'), may hold values from 0 to 8191
- tile_items: int32 [16, 8, 4096], P('ublk', 'salt'), may hold values from 0 to 511
- tile_weight: float32 [16, 8, 4096], P('ublk', 'salt'), may hold values from 0.5 to 8
- live_count: int32 [16, 8], P('ublk', 'salt'), may hold values from 2048 to 4096, as said below
Outputs:
- item_factors: float32 [8, 512, 256], P('salt', 'ublk')
- residual: float32 [8, 512, 256], P('salt', 'ublk')
Inputs may be any that keep to these rules, and one draw needn't show every extreme that they name: Every entry of live_count is at least 2048 and at most 4096; some tile is full.
All inputs are finite; a program needn't handle non-finite values.
Results may differ from a plain program's by a relative error of at most 0.0022.
Values may be sent and summed in bfloat16 or wider, within the bound.
A program may use at most 64 MiB of HBM per device.

v0:
```python
import jax
import jax.numpy as jnp
from jax import lax
from jax.sharding import PartitionSpec as P

ITERS = 8
ITEM_DEV = 32


REG = 1.0
EPS = 1e-06


def conjugate(rhs, image_of):
    solution = jnp.zeros_like(rhs)
    resid = rhs
    direction = rhs
    norm_now = jnp.sum(resid * resid, axis=1)
    for step in range(ITERS):
        image = image_of(direction)
        alpha = norm_now / (jnp.sum(direction * image, axis=1) + EPS)
        solution = solution + alpha[:, None] * direction
        resid = resid - alpha[:, None] * image
        norm_next = jnp.sum(resid * resid, axis=1)
        direction = resid + (norm_next / (norm_now + EPS))[:, None] * direction
        norm_now = norm_next
    return (solution, resid)


def body(user_factors, tile_users, tile_items, tile_weight, live_count):
    shard = user_factors[0]
    block = lax.all_gather(shard, "salt", axis=0, tiled=True)
    contract = (((0,), (0,)), ((), ()))
    own_gram = lax.dot_general(shard, shard, contract, preferred_element_type=jnp.float32)
    gram = lax.psum(own_gram, ("ublk", "salt"))
    users = tile_users[0, 0]
    items = tile_items[0, 0]
    raw = tile_weight[0, 0]
    live = jnp.arange(users.shape[0], dtype=jnp.int32) < live_count[0, 0]
    weight = jnp.where(live, raw, jnp.zeros_like(raw))
    confid = jnp.where(live, 1.0 + raw, jnp.zeros_like(raw))
    rows = jnp.take(block, users, axis=0).astype(jnp.float32)
    column_items = ITEM_DEV * lax.axis_size("ublk")
    rhs_terms = jax.ops.segment_sum(confid[:, None] * rows, items, num_segments=column_items)

    def local_terms(whole_dir):
        along = jnp.sum(rows * whole_dir[items], axis=1) * weight
        return jax.ops.segment_sum(along[:, None] * rows, items, num_segments=column_items)

    def finish(summed, direction):
        return summed + jnp.dot(direction, gram, precision=lax.Precision.HIGHEST) + REG * direction

    rhs = lax.psum(rhs_terms, "ublk")

    def image_every(direction):
        summed = lax.psum(local_terms(direction), "ublk")
        return finish(summed, direction)

    solution_all, resid_all = conjugate(rhs, image_every)
    start = lax.axis_index("ublk") * ITEM_DEV
    solution = lax.dynamic_slice_in_dim(solution_all, start, ITEM_DEV, 0)
    resid = lax.dynamic_slice_in_dim(resid_all, start, ITEM_DEV, 0)
    return (solution[None], resid[None])


def solution(mesh):
    return jax.shard_map(
        body,
        mesh=mesh,
        in_specs=(
            P("ublk", "salt", None),
            P("ublk", "salt", None),
            P("ublk", "salt", None),
            P("ublk", "salt", None),
            P("ublk", "salt"),
        ),
        out_specs=(P("salt", "ublk", None), P("salt", "ublk", None)),
        check_vma=False,
    )
```

profile of v0, /device:TPU:0, one launch (start us, length us, event | category | flops | bytes accessed | tf_op | source)
XLA Modules:
  0.0 1353.0 jit_solution(7503660293953594438)
XLA Ops:
  10.8 33.5 %all-gather.3.cloned.1.call-done = bf16[1,8192,256]{2,1,0:T(8,128)(2,1)} async-done(((bf16[1,1024,256]{2,1,0:T(8,128)(2,1)}), bf16[1,8192,256]{2,1,0:T(8,128)(2,1)}) %all-gather.3.cloned.1.call-update) | async-done | bytes 4194320 | tf_op jit(solution)/shard_map/all_gather | solution.py:32
  44.3 15.8 %gather_fusion = bf16[4096,256]{1,0:T(8,128)(2,1)S(1)} fusion(bf16[8192,256]{1,0:T(8,128)(2,1)} %bitcast.43, s32[4096]{0:T(1024)S(1)} %broadcast_clamp_fusion.1), kind=kCustom, calls=%fused_computation | custom fusion | bytes 4210688 | tf_op jit(solution)/shard_map/jit(_take)/gather | solution.py:42
  60.1 26.1 %scatter_custom_fusion = f32[512,256]{1,0:T(8,128)} fusion(s32[4096]{0:T(1024)S(1)} %bitcast.56, f32[4096]{0:T(1024)S(1)} %add_select_fusion, f32[]{:T(128)} %constant.11.clone.1, bf16[4096,256]{1,0:T(8,128)(2,1)S(1)} %gather_fusion, pred[4096]{0:T(1024)(128)(4,1)S(1)} %compare_and_fusion), kind=kCustom, calls=%fused_computation.35 | custom fusion | flops 4194304 | bytes 2641924 | tf_op jit(solution)/shard_map/scatter-add | solution.py:44
  87.4 84.7 %all-reduce.11.cloned.1.call-done = f32[512,256]{1,0:T(8,128)} async-done(((f32[512,256]{1,0:T(8,128)}), f32[512,256]{1,0:T(8,128)}) %all-reduce.11.cloned.1.call-update) | async-done | bytes 524304 | tf_op jit(solution)/shard_map/psum | solution.py:53
  172.1 17.1 %gather_fusion.1 = f32[4096,256]{1,0:T(8,128)} fusion(f32[512,256]{1,0:T(8,128)} %all-reduce.11.cloned.1.call-done, s32[4096]{0:T(1024)S(1)} %broadcast_clamp_fusion), kind=kCustom, calls=%fused_computation.1 | custom fusion | bytes 8404992 | tf_op jit(solution)/shard_map/gather | solution.py:47
  192.2 26.1 %scatter_custom_fusion.1 = f32[512,256]{1,0:T(8,128)} fusion(s32[4096]{0:T(1024)S(1)} %bitcast.57, f32[4096]{0:T(1024)S(1)} %fusion.60, f32[]{:T(128)} %constant.11.clone.1, bf16[4096,256]{1,0:T(8,128)(2,1)S(1)} %gather_fusion, pred[4096]{0:T(1024)(128)(4,1)S(1)} %compare_and_fusion), kind=kCustom, calls=%fused_computation.37 | custom fusion | flops 4194304 | bytes 2641924 | tf_op jit(solution)/shard_map/scatter-add | solution.py:48
  218.9 100.4 %all-reduce.15.cloned.1.call-done = f32[256,256]{1,0:T(8,128)} async-done(((f32[256,256]{1,0:T(8,128)}), f32[256,256]{1,0:T(8,128)}) %all-reduce.15.cloned.1.call-update) | async-done | bytes 262160 | tf_op jit(solution)/shard_map/psum | solution.py:35
  319.4 86.2 %all-reduce.13.cloned.1.call-done = f32[512,256]{1,0:T(8,128)} async-done(((f32[512,256]{1,0:T(8,128)}), f32[512,256]{1,0:T(8,128)}) %all-reduce.13.cloned.1.call-update) | async-done | bytes 524304 | tf_op jit(solution)/shard_map/psum | solution.py:56
  408.4 16.1 %gather_fusion.2 = f32[4096,256]{1,0:T(8,128)} fusion(f32[512,256]{1,0:T(8,128)S(1)} %multiply_add_fusion.7, s32[4096]{0:T(1024)S(1)} %broadcast_clamp_fusion), kind=kCustom, calls=%fused_computation.2 | custom fusion | bytes 8404992 | tf_op jit(solution)/shard_map/gather | solution.py:47
  427.5 26.1 %scatter_custom_fusion.2 = f32[512,256]{1,0:T(8,128)} fusion(s32[4096]{0:T(1024)S(1)} %bitcast.58, f32[4096]{0:T(1024)S(1)} %fusion.59, f32[]{:T(128)} %constant.11.clone.1, bf16[4096,256]{1,0:T(8,128)(2,1)S(1)} %gather_fusion, pred[4096]{0:T(1024)(128)(4,1)S(1)} %compare_and_fusion), kind=kCustom, calls=%fused_computation.39 | custom fusion | flops 4194304 | bytes 2641924 | tf_op jit(solution)/shard_map/scatter-add | solution.py:48
  453.7 85.3 %all-reduce.17.cloned.1.call-done = f32[512,256]{1,0:T(8,128)} async-done(((f32[512,256]{1,0:T(8,128)}), f32[512,256]{1,0:T(8,128)}) %all-reduce.17.cloned.1.call-update) | async-done | bytes 524304 | tf_op jit(solution)/shard_map/psum | solution.py:56
  542.9 16.1 %gather_fusion.3 = f32[4096,256]{1,0:T(8,128)} fusion(f32[512,256]{1,0:T(8,128)S(1)} %multiply_add_fusion.5, s32[4096]{0:T(1024)S(1)} %broadcast_clamp_fusion), kind=kCustom, calls=%fused_computation.3 | custom fusion | bytes 8404992 | tf_op jit(solution)/shard_map/gather | solution.py:47
  559.0 3.5 fusion.5
  562.5 26.5 %scatter_custom_fusion.3 = f32[512,256]{1,0:T(8,128)} fusion(s32[4096]{0:T(1024)S(1)} %bitcast.59, f32[4096]{0:T(1024)S(1)} %fusion.58, f32[]{:T(128)} %constant.11.clone.1, bf16[4096,256]{1,0:T(8,128)(2,1)} %copy-done.1, pred[4096]{0:T(1024)(128)(4,1)S(1)} %compare_and_fusion), kind=kCustom, calls=%fused_computation.41 | custom fusion | flops 4194304 | bytes 2641924 | tf_op jit(solution)/shard_map/scatter-add | solution.py:48
  589.2 85.1 %all-reduce.19.cloned.1.call-done = f32[512,256]{1,0:T(8,128)} async-done(((f32[512,256]{1,0:T(8,128)}), f32[512,256]{1,0:T(8,128)}) %all-reduce.19.cloned.1.call-update) | async-done | bytes 524304 | tf_op jit(solution)/shard_map/psum | solution.py:56
  677.4 16.1 %gather_fusion.4 = f32[4096,256]{1,0:T(8,128)} fusion(f32[512,256]{1,0:T(8,128)S(1)} %get-tuple-element.18, s32[4096]{0:T(1024)S(1)} %broadcast_clamp_fusion), kind=kCustom, calls=%fused_computation.4 | custom fusion | bytes 8404992 | tf_op jit(solution)/shard_map/gather | solution.py:47
  696.5 26.1 %scatter_custom_fusion.4 = f32[512,256]{1,0:T(8,128)} fusion(s32[4096]{0:T(1024)S(1)} %bitcast.60, f32[4096]{0:T(1024)S(1)} %fusion.57, f32[]{:T(128)} %constant.11.clone.1, bf16[4096,256]{1,0:T(8,128)(2,1)S(1)} %copy-done.2, pred[4096]{0:T(1024)(128)(4,1)S(1)} %compare_and_fusion), kind=kCustom, calls=%fused_computation.43 | custom fusion | flops 4194304 | bytes 2641924 | tf_op jit(solution)/shard_map/scatter-add | solution.py:48
  722.7 85.2 %all-reduce.21.cloned.1.call-done = f32[512,256]{1,0:T(8,128)} async-done(((f32[512,256]{1,0:T(8,128)}), f32[512,256]{1,0:T(8,128)}) %all-reduce.21.cloned.1.call-update) | async-done | bytes 524304 | tf_op jit(solution)/shard_map/psum | solution.py:56
  810.7 16.1 %gather_fusion.5 = f32[4096,256]{1,0:T(8,128)} fusion(f32[512,256]{1,0:T(8,128)S(1)} %multiply_add_fusion.3, s32[4096]{0:T(1024)S(1)} %broadcast_clamp_fusion), kind=kCustom, calls=%fused_computation.5 | custom fusion | bytes 8404992 | tf_op jit(solution)/shard_map/gather | solution.py:47
  829.8 26.1 %scatter_custom_fusion.5 = f32[512,256]{1,0:T(8,128)} fusion(s32[4096]{0:T(1024)S(1)} %bitcast.61, f32[4096]{0:T(1024)S(1)} %fusion.56, f32[]{:T(128)} %constant.11.clone.1, bf16[4096,256]{1,0:T(8,128)(2,1)S(1)} %copy-done.2, pred[4096]{0:T(1024)(128)(4,1)S(1)} %compare_and_fusion), kind=kCustom, calls=%fused_computation.45 | custom fusion | flops 4194304 | bytes 2641924 | tf_op jit(solution)/shard_map/scatter-add | solution.py:48
  856.2 85.0 %all-reduce.23.cloned.1.call-done = f32[512,256]{1,0:T(8,128)} async-done(((f32[512,256]{1,0:T(8,128)}), f32[512,256]{1,0:T(8,128)}) %all-reduce.23.cloned.1.call-update) | async-done | bytes 524304 | tf_op jit(solution)/shard_map/psum | solution.py:56
  944.4 16.1 %gather_fusion.6 = f32[4096,256]{1,0:T(8,128)} fusion(f32[512,256]{1,0:T(8,128)S(1)} %multiply_add_fusion.2, s32[4096]{0:T(1024)S(1)} %broadcast_clamp_fusion), kind=kCustom, calls=%fused_computation.6 | custom fusion | bytes 8404992 | tf_op jit(solution)/shard_map/gather | solution.py:47
  960.4 3.5 fusion.11
  963.9 26.5 %scatter_custom_fusion.6 = f32[512,256]{1,0:T(8,128)} fusion(s32[4096]{0:T(1024)S(1)} %bitcast.62, f32[4096]{0:T(1024)S(1)} %fusion.55, f32[]{:T(128)} %constant.11.clone.1, bf16[4096,256]{1,0:T(8,128)(2,1)} %copy-done.1, pred[4096]{0:T(1024)(128)(4,1)S(1)} %compare_and_fusion), kind=kCustom, calls=%fused_computation.47 | custom fusion | flops 4194304 | bytes 2641924 | tf_op jit(solution)/shard_map/scatter-add | solution.py:48
  990.5 85.3 %all-reduce.25.cloned.1.call-done = f32[512,256]{1,0:T(8,128)} async-done(((f32[512,256]{1,0:T(8,128)}), f32[512,256]{1,0:T(8,128)}) %all-reduce.25.cloned.1.call-update) | async-done | bytes 524304 | tf_op jit(solution)/shard_map/psum | solution.py:56
  1077.9 16.1 %gather_fusion.7 = f32[4096,256]{1,0:T(8,128)} fusion(f32[512,256]{1,0:T(8,128)S(1)} %multiply_add_fusion.1, s32[4096]{0:T(1024)S(1)} %broadcast_clamp_fusion), kind=kCustom, calls=%fused_computation.7 | custom fusion | bytes 8404992 | tf_op jit(solution)/shard_map/gather | solution.py:47
  1094.0 3.5 fusion.13
  1097.5 26.5 %scatter_custom_fusion.7 = f32[512,256]{1,0:T(8,128)} fusion(s32[4096]{0:T(1024)S(1)} %bitcast.63, f32[4096]{0:T(1024)S(1)} %fusion.54, f32[]{:T(128)} %constant.11.clone.1, bf16[4096,256]{1,0:T(8,128)(2,1)} %copy-done.1, pred[4096]{0:T(1024)(128)(4,1)S(1)} %compare_and_fusion), kind=kCustom, calls=%fused_computation.49 | custom fusion | flops 4194304 | bytes 2641924 | tf_op jit(solution)/shard_map/scatter-add | solution.py:48
  1124.3 85.0 %all-reduce.27.cloned.1.call-done = f32[512,256]{1,0:T(8,128)} async-done(((f32[512,256]{1,0:T(8,128)}), f32[512,256]{1,0:T(8,128)}) %all-reduce.27.cloned.1.call-update) | async-done | bytes 524304 | tf_op jit(solution)/shard_map/psum | solution.py:56
  1211.5 16.1 %gather_fusion.8 = f32[4096,256]{1,0:T(8,128)} fusion(f32[512,256]{1,0:T(8,128)S(1)} %multiply_add_fusion, s32[4096]{0:T(1024)S(1)} %broadcast_clamp_fusion), kind=kCustom, calls=%fused_computation.8 | custom fusion | bytes 8404992 | tf_op jit(solution)/shard_map/gather | solution.py:47
  1231.1 26.5 %scatter_custom_fusion.8 = f32[512,256]{1,0:T(8,128)} fusion(s32[4096]{0:T(1024)S(1)} %bitcast.64, f32[4096]{0:T(1024)S(1)} %fusion.53, f32[]{:T(128)} %constant.11.clone.1, bf16[4096,256]{1,0:T(8,128)(2,1)} %copy-done.1, pred[4096]{0:T(1024)(128)(4,1)S(1)} %compare_and_fusion), kind=kCustom, calls=%fused_computation.51 | custom fusion | flops 4194304 | bytes 2641924 | tf_op jit(solution)/shard_map/scatter-add | solution.py:48
  1257.9 85.0 %all-reduce.29.cloned.1.call-done = f32[512,256]{1,0:T(8,128)} async-done(((f32[512,256]{1,0:T(8,128)}), f32[512,256]{1,0:T(8,128)}) %all-reduce.29.cloned.1.call-update) | async-done | bytes 524304 | tf_op jit(solution)/shard_map/psum | solution.py:56
  (107 shorter events, 44.8 us)
Async XLA Ops:
  7.2 37.1 %all-gather.3.cloned.1.call-start = ((), (), s32[]{:S(2)}) async-start(), calls=%async_computation.10 | async-start | bytes 4718592 | tf_op jit(solution)/shard_map/all_gather | solution.py:32
  7.9 164.2 %all-reduce.11.cloned.1.call-start = ((), (), s32[]{:S(2)}) async-start(), calls=%async_computation | async-start | bytes 1048576 | tf_op jit(solution)/shard_map/psum | solution.py:53
  44.3 15.8 %copy-start.10 = (s32[1,1,4096]{2,1,0:T(1,128)S(1)}, s32[1,1,4096]{2,1,0:T(1,128)}, u32[]{:S(2)}) copy-start(s32[1,1,4096]{2,1,0:T(1,128)} %param.7) | copy-start | bytes 49156
  44.3 42.0 %copy-start.9 = (bf16[1,1024,256]{2,1,0:T(8,128)(2,1)S(1)}, bf16[1,1024,256]{2,1,0:T(8,128)(2,1)}, u32[]{:S(2)}) copy-start(bf16[1,1024,256]{2,1,0:T(8,128)(2,1)} %param.5) | copy-start | bytes 1572868
  60.1 367.4 %copy-start.1 = (bf16[4096,256]{1,0:T(8,128)(2,1)}, bf16[4096,256]{1,0:T(8,128)(2,1)S(1)}, u32[]{:S(2)}) copy-start(bf16[4096,256]{1,0:T(8,128)(2,1)S(1)} %gather_fusion) | copy-start | bytes 6291460
  86.2 233.2 %all-reduce.15.cloned.1.call-start = ((), (), s32[]{:S(2)}) async-start(), calls=%async_computation.2 | async-start | bytes 524288 | tf_op jit(solution)/shard_map/psum | solution.py:35
  87.3 318.2 %all-reduce.13.cloned.1.call-start = ((), (), s32[]{:S(2)}) async-start(), calls=%async_computation.1 | async-start | bytes 1048576 | tf_op jit(solution)/shard_map/psum | solution.py:56
  189.2 3.0 copy-start.8
  189.2 216.4 %copy-start = (f32[512,256]{1,0:T(8,128)S(1)}, f32[512,256]{1,0:T(8,128)}, u32[]{:S(2)}) copy-start(f32[512,256]{1,0:T(8,128)} %all-reduce.11.cloned.1.call-done) | copy-start | bytes 1572868
  218.4 320.6 %all-reduce.17.cloned.1.call-start = ((), (), s32[]{:S(2)}) async-start(), calls=%async_computation.3 | async-start | bytes 1048576 | tf_op jit(solution)/shard_map/psum | solution.py:56
  407.4 0.8 copy-start.4
  424.5 114.5 %copy-start.3 = (f32[256,256]{1,0:T(8,128)S(1)}, f32[256,256]{1,0:T(8,128)}, u32[]{:S(2)}) copy-start(f32[256,256]{1,0:T(8,128)} %all-reduce.15.cloned.1.call-done) | copy-start | bytes 786436
  453.6 220.7 %all-reduce.19.cloned.1.call-start = ((), (), s32[]{:S(2)}) async-start(), calls=%async_computation.4 | async-start | bytes 1048576 | tf_op jit(solution)/shard_map/psum | solution.py:56
  589.0 218.8 %all-reduce.21.cloned.1.call-start = ((), (), s32[]{:S(2)}) async-start(), calls=%async_computation.5 | async-start | bytes 1048576 | tf_op jit(solution)/shard_map/psum | solution.py:56
  676.3 1.0 copy-start.6
  677.4 16.1 %copy-start.2 = (bf16[4096,256]{1,0:T(8,128)(2,1)S(1)}, bf16[4096,256]{1,0:T(8,128)(2,1)}, u32[]{:S(2)}) copy-start(bf16[4096,256]{1,0:T(8,128)(2,1)} %copy-done.1) | copy-start | bytes 6291460
  693.5 116.1 %copy-start.7 = (f32[512,256]{1,0:T(8,128)S(1)}, f32[512,256]{1,0:T(8,128)}, u32[]{:S(2)}) copy-start(f32[512,256]{1,0:T(8,128)} %copy-done.6) | copy-start | bytes 1572868
  722.6 218.6 %all-reduce.23.cloned.1.call-start = ((), (), s32[]{:S(2)}) async-start(), calls=%async_computation.6 | async-start | bytes 1048576 | tf_op jit(solution)/shard_map/psum | solution.py:56
  809.8 0.8 copy-start.5
  855.9 219.9 %all-reduce.25.cloned.1.call-start = ((), (), s32[]{:S(2)}) async-start(), calls=%async_computation.7 | async-start | bytes 1048576 | tf_op jit(solution)/shard_map/psum | solution.py:56
  990.5 218.9 %all-reduce.27.cloned.1.call-start = ((), (), s32[]{:S(2)}) async-start(), calls=%async_computation.8 | async-start | bytes 1048576 | tf_op jit(solution)/shard_map/psum | solution.py:56
  1124.0 218.9 %all-reduce.29.cloned.1.call-start = ((), (), s32[]{:S(2)}) async-start(), calls=%async_computation.9 | async-start | bytes 1048576 | tf_op jit(solution)/shard_map/psum | solution.py:56
Sparse Core Ops, SparseCore 0:
  9.7 34.5 all-gather.2
  86.3 85.7 all-reduce.10
  176.8 142.4 all-reduce.14
  322.4 83.0 all-reduce.12
  453.8 85.1 all-reduce.16
  589.1 85.1 all-reduce.18
  722.8 85.0 all-reduce.20
  856.0 85.1 all-reduce.22
  990.6 85.1 all-reduce.24
  1124.2 85.1 all-reduce.26
  1257.7 85.1 all-reduce.28
where the time goes:
time: 1360 us; the launch traced here: 1350 us
  waiting for transfers between devices  902 us (66%)
  other arithmetic  273 us (20%)
  local copies, waits for them, and re-layouts  147 us (11%)
  between operations  15.1 us (1%)
  matrix products  14.8 us (1%)
    psum x8, waiting for transfers between devices, image_every(): summed = lax.psum(local_terms(direction), 'ublk')  682 us
    scatter-add x8, other arithmetic, local_terms(): jax.ops.segment_sum(along[:, None] * rows, items, num_segments=column_items)  210 us
    gather x8, local copies, waits for them, and re-layouts, local_terms(): along = jnp.sum(rows * whole_dir[items], axis=1) * weight  130 us
    psum x1, waiting for transfers between devices, body(): gram = lax.psum(own_gram, ('ublk', 'salt'))  100 us
    psum x1, waiting for transfers between devices, body(): rhs = lax.psum(rhs_terms, 'ublk')  84.7 us
    all_gather x1, waiting for transfers between devices, body(): block = lax.all_gather(shard, 'salt', axis=0, tiled=True)  33.5 us
  transfers between devices with their start and end apart: 11, of which 11 were waited for; matrix products, arithmetic and copies ran while one was open for 4% of the time, Pallas kernels for 0%

commit v1 on v0

v1 whole, which is shorter than its diff:
```python
import jax
import jax.numpy as jnp
from jax import lax
from jax.experimental import pallas as pl
from jax.experimental.pallas import tpu as pltpu
from jax.sharding import PartitionSpec as P

ITERS = 8
REG = 1.0
EPS = 1e-06

X = 4
OWNERS = X * X
OWN = 32
RANK = 256
ITEMS = OWNERS * OWN
SLOTS = 4096
SHARD = 1024
SALT = 8
CHUNKS = 4
CHUNK = SHARD // CHUNKS
TILE = 1024
GRAM_OWN = RANK // OWNERS

F32 = jnp.float32
BF16 = jnp.bfloat16
MESH = pl.DeviceIdType.MESH


def ring(a):
    return min(a, X - a)


OFFSETS = sorted(
    [(dx, dz) for dx in range(X) for dz in range(X)],
    key=lambda o: (ring(o[0]) + ring(o[1]), o),
)
FAR_FIRST = list(range(OWNERS - 1, 0, -1))
GROUPS = [list(range(OWNERS))]

PARTNER, UP, DOWN, ACROSS, P_UP, P_DOWN, P_ACROSS = range(7)


def kernel(
    shard, users, items, raw, live,
    x_out, r_out,
    block, rows_t, scaled_t, rows, mask, terms, gram, gram_sum, gram_in, gram_own,
    rhs, rhs_in, whole_dir, direction, own_terms, out_terms, in_terms,
    ag_send, ag_recv, gram_send, gram_recv, gall_send, gall_recv,
    rhs_send, rhs_recv, dir_send, dir_recv, loc_send, loc_recv,
):
    ublk = lax.axis_index("ublk")
    salt = lax.axis_index("salt")
    px, pz = lax.div(ublk, X), lax.rem(ublk, X)
    py, pc = lax.div(salt, 2), lax.rem(salt, 2)

    def owner(k, sign=1):
        dx, dz = OFFSETS[k]
        return lax.rem(px + sign * dx + X, X) * X + lax.rem(pz + sign * dz + X, X)

    def line(dy, core):
        return lax.rem(py + dy, X) * 2 + core

    def remote(src, dst, send, recv, device):
        copy = pltpu.make_async_remote_copy(
            src_ref=src, dst_ref=dst, send_sem=send, recv_sem=recv,
            device_id=device, device_id_type=MESH,
        )
        return copy

    barrier = pltpu.get_barrier_semaphore()
    peers = [(owner(k), salt) for k in range(1, OWNERS)]
    peers += [(ublk, line(1, pc)), (ublk, line(3, pc)), (ublk, line(0, 1 - pc))]
    for device in peers:
        pl.semaphore_signal(barrier, inc=1, device_id=device, device_id_type=MESH)
    pl.semaphore_wait(barrier, len(peers))

    def piece(ref, h):
        return ref.at[pl.ds(h * CHUNK, CHUNK)]

    def gathered(src, place, h, device):
        return remote(src, piece(block.at[place], h), ag_send.at[place, h], ag_recv.at[place, h], device)

    copies = {}
    for h in range(CHUNKS):
        copies[UP, h] = gathered(piece(shard, h), UP, h, (ublk, line(1, pc)))
        copies[DOWN, h] = gathered(piece(shard, h), DOWN, h, (ublk, line(3, pc)))
        copies[PARTNER, h] = gathered(piece(shard, h), PARTNER, h, (ublk, line(0, 1 - pc)))
        for place in (UP, DOWN, PARTNER):
            copies[place, h].start()

    def relay(h):
        for place in (UP, DOWN):
            copies[place, h].wait_recv()
        copies[ACROSS, h] = gathered(piece(block.at[UP + pc], h), ACROSS, h, (ublk, line(1 + 2 * pc, pc)))
        copies[P_UP, h] = gathered(piece(block.at[UP], h), P_UP, h, (ublk, line(0, 1 - pc)))
        copies[P_DOWN, h] = gathered(piece(block.at[DOWN], h), P_DOWN, h, (ublk, line(0, 1 - pc)))
        for place in (ACROSS, P_UP, P_DOWN):
            copies[place, h].start()

    def relay_across(h):
        copies[ACROSS, h].wait_recv()
        copies[P_ACROSS, h] = gathered(piece(block.at[ACROSS], h), P_ACROSS, h, (ublk, line(0, 1 - pc)))
        copies[P_ACROSS, h].start()

    def arrived(place):
        for h in range(CHUNKS):
            copies[place, h].wait_recv()

    def select(source, who, first=False):
        part = source[...]
        part_t = part.T
        outer = jnp.dot(part_t, part, preferred_element_type=F32)
        if first:
            gram[...] = outer
        else:
            gram[...] += outer
        base = who * SHARD

        def step(n, carry):
            at = pl.ds(pl.multiple_of(n * TILE, TILE), TILE)
            place = users[:, at] - base
            chosen = place == lax.broadcasted_iota(jnp.int32, (SHARD, TILE), 0)
            one_hot = jnp.where(chosen, 1.0, 0.0).astype(BF16)
            found = jnp.dot(part_t, one_hot, preferred_element_type=F32).astype(BF16)
            if first:
                rows_t[:, at] = found
            else:
                rows_t[:, at] += found
            return carry

        lax.fori_loop(0, SLOTS // TILE, step, 0)

    select(shard, salt, first=True)
    arrived(PARTNER)
    select(block.at[PARTNER], line(0, 1 - pc))
    for h in range(CHUNKS // 2):
        relay(h)
    for k in range(OWNERS):
        place = items[...] - owner(k) * OWN
        chosen = place == lax.broadcasted_iota(jnp.int32, (OWN, SLOTS), 0)
        mask[pl.ds(k * OWN, OWN)] = jnp.where(chosen, 1.0, 0.0).astype(BF16)
    for h in range(CHUNKS // 2, CHUNKS):
        relay(h)
    select(block.at[UP], line(3, pc))
    select(block.at[DOWN], line(1, pc))
    for h in range(CHUNKS // 2):
        relay_across(h)
    arrived(P_UP)
    select(block.at[P_UP], line(3, 1 - pc))
    for h in range(CHUNKS // 2, CHUNKS):
        relay_across(h)
    arrived(P_DOWN)
    select(block.at[P_DOWN], line(1, 1 - pc))
    select(block.at[ACROSS], line(2, pc))
    arrived(P_ACROSS)
    select(block.at[P_ACROSS], line(2, 1 - pc))

    gram_copies = [
        remote(
            gram.at[pl.ds(pl.multiple_of(owner(k) * GRAM_OWN, GRAM_OWN), GRAM_OWN)], gram_in.at[k],
            gram_send.at[k], gram_recv.at[k], (owner(k), salt),
        )
        for k in range(OWNERS) if k
    ]
    for copy in reversed(gram_copies):
        copy.start()

    alive = lax.broadcasted_iota(jnp.int32, (1, SLOTS), 1) < live[0, 0]
    weight = jnp.where(alive, raw[...], 0.0)
    confid = jnp.where(alive, 1.0 + raw[...], 0.0)
    for n in range(SLOTS // TILE):
        at = pl.ds(n * TILE, TILE)
        rows[at] = rows_t[:, at].T
        scaled_t[:, at] = (rows_t[:, at].astype(F32) * weight[:, n * TILE:(n + 1) * TILE]).astype(BF16)

    upper = confid.astype(BF16)
    lower = (confid - upper.astype(F32)).astype(BF16)
    for step, level in enumerate((upper, lower)):
        for n in range(SLOTS // TILE):
            at = pl.ds(n * TILE, TILE)
            terms[:, at] = jnp.where(mask[:, at] != 0, level[:, n * TILE:(n + 1) * TILE], jnp.zeros((), BF16))
        part = jnp.dot(terms[...], rows[...], preferred_element_type=F32)
        if step == 0:
            rhs[...] = part
        else:
            rhs[...] += part

    rhs_copies = [
        remote(
            rhs.at[pl.ds(k * OWN, OWN)], rhs_in.at[k], rhs_send.at[k], rhs_recv.at[k], (owner(k), salt)
        )
        for k in range(OWNERS) if k
    ]
    for copy in reversed(rhs_copies):
        copy.start()

    own_rows = pl.ds(pl.multiple_of(ublk * GRAM_OWN, GRAM_OWN), GRAM_OWN)
    total = gram[own_rows]
    for k in range(1, OWNERS):
        gram_copies[k - 1].wait_recv()
        total = total + gram_in[k]
    gram_own[...] = total
    gram_sum[own_rows] = total
    gall_copies = [
        remote(
            gram_own, gram_sum.at[own_rows], gall_send.at[k], gall_recv.at[k], (owner(k), salt)
        )
        for k in range(OWNERS) if k
    ]
    for copy in reversed(gall_copies):
        copy.start()

    total = rhs[pl.ds(0, OWN)]
    for k in range(1, OWNERS):
        rhs_copies[k - 1].wait_recv()
        total = total + rhs_in[k]
    direction[...] = total
    r_out[...] = total
    x_out[...] = jnp.zeros_like(total)
    whole_dir[pl.ds(0, OWN)] = total.astype(BF16)

    def iteration(t, carry):
        dir_copies = {
            k: remote(
                whole_dir.at[pl.ds(0, OWN)], whole_dir.at[pl.ds(k * OWN, OWN)],
                dir_send.at[k], dir_recv.at[k], (owner(k, -1), salt),
            )
            for k in range(1, OWNERS)
        }
        loc_copies = {
            k: remote(
                out_terms.at[pl.ds(k * OWN, OWN)], in_terms.at[k],
                loc_send.at[k], loc_recv.at[k], (owner(k), salt),
            )
            for k in range(1, OWNERS)
        }
        for k in FAR_FIRST:
            dir_copies[k].start()
        for group in GROUPS:
            for k in group:
                if k:
                    dir_copies[k].wait_recv()
            at = pl.ds(group[0] * OWN, len(group) * OWN)
            for n in range(SLOTS // TILE):
                cols = pl.ds(n * TILE, TILE)
                along = jnp.dot(whole_dir[at], scaled_t[:, cols], preferred_element_type=F32)
                terms[at, cols] = jnp.where(mask[at, cols] != 0, along.astype(BF16), jnp.zeros((), BF16))
            local = jnp.dot(terms[at], rows[...], preferred_element_type=F32)
            if group[0] == 0:
                own_terms[...] = local[:OWN]
            out_terms[at] = local.astype(BF16)
            for k in reversed(group):
                if k:
                    loc_copies[k].start()

        @pl.when(t == 0)
        def _():
            for copy in gall_copies:
                copy.wait_recv()

        p = direction[...]
        r = r_out[...]
        norm_now = jnp.sum(r * r, axis=1, keepdims=True)
        image = jnp.dot(p, gram_sum[...], precision=lax.Precision.HIGHEST, preferred_element_type=F32) + REG * p
        image = image + own_terms[...]
        for k in range(1, OWNERS):
            dir_copies[k].wait_send()
        for k in range(1, OWNERS):
            loc_copies[k].wait_recv()
            image = image + in_terms[k].astype(F32)
        alpha = norm_now / (jnp.sum(p * image, axis=1, keepdims=True) + EPS)
        x_out[...] += alpha * p
        r = r - alpha * image
        r_out[...] = r
        norm_next = jnp.sum(r * r, axis=1, keepdims=True)
        p = r + (norm_next / (norm_now + EPS)) * p
        direction[...] = p
        whole_dir[pl.ds(0, OWN)] = p.astype(BF16)
        for k in range(1, OWNERS):
            loc_copies[k].wait_send()
        return carry

    lax.fori_loop(0, ITERS, iteration, 0)

    for copy in list(copies.values()) + gram_copies + gall_copies + rhs_copies:
        copy.wait_send()


def body(user_factors, tile_users, tile_items, tile_weight, live_count):
    vmem = pl.BlockSpec(memory_space=pltpu.VMEM)
    dma = pltpu.SemaphoreType.DMA
    found, left = pl.pallas_call(
        kernel,
        name="als_cg",
        out_shape=(jax.ShapeDtypeStruct((OWN, RANK), F32), jax.ShapeDtypeStruct((OWN, RANK), F32)),
        in_specs=[vmem, vmem, vmem, vmem, pl.BlockSpec(memory_space=pltpu.SMEM)],
        out_specs=(vmem, vmem),
        scratch_shapes=[
            pltpu.VMEM((SALT - 1, SHARD, RANK), BF16),
            pltpu.VMEM((RANK, SLOTS), BF16),
            pltpu.VMEM((RANK, SLOTS), BF16),
            pltpu.VMEM((SLOTS, RANK), BF16),
            pltpu.VMEM((ITEMS, SLOTS), BF16),
            pltpu.VMEM((ITEMS, SLOTS), BF16),
            pltpu.VMEM((RANK, RANK), F32),
            pltpu.VMEM((RANK, RANK), F32),
            pltpu.VMEM((OWNERS, GRAM_OWN, RANK), F32),
            pltpu.VMEM((GRAM_OWN, RANK), F32),
            pltpu.VMEM((ITEMS, RANK), F32),
            pltpu.VMEM((OWNERS, OWN, RANK), F32),
            pltpu.VMEM((ITEMS, RANK), BF16),
            pltpu.VMEM((OWN, RANK), F32),
            pltpu.VMEM((OWN, RANK), F32),
            pltpu.VMEM((ITEMS, RANK), BF16),
            pltpu.VMEM((OWNERS, OWN, RANK), BF16),
            dma((SALT - 1, CHUNKS)), dma((SALT - 1, CHUNKS)),
            dma((OWNERS,)), dma((OWNERS,)), dma((OWNERS,)), dma((OWNERS,)),
            dma((OWNERS,)), dma((OWNERS,)), dma((OWNERS,)), dma((OWNERS,)),
            dma((OWNERS,)), dma((OWNERS,)),
        ],
        compiler_params=pltpu.CompilerParams(
            collective_id=0, has_side_effects=True, vmem_limit_bytes=56 * 2**20
        ),
    )(user_factors[0], tile_users[0], tile_items[0], tile_weight[0], live_count)
    return (found[None], left[None])


def solution(mesh):
    return jax.shard_map(
        body,
        mesh=mesh,
        in_specs=(
            P("ublk", "salt", None),
            P("ublk", "salt", None),
            P("ublk", "salt", None),
            P("ublk", "salt", None),
            P("ublk", "salt"),
        ),
        out_specs=(P("salt", "ublk", None), P("salt", "ublk", None)),
        check_vma=False,
    )
```

time: 1360 us -> 171 us (0.13)
  waiting for transfers between devices: 902 us -> 0 us
  other arithmetic: 273 us -> 0 us
  Pallas kernels: 0 us -> 168 us
  local copies, waits for them, and re-layouts: 147 us -> 2 us
  matrix products: 14.8 us -> 0 us
  between operations: 15.1 us -> 1.29 us
    psum x10 -> x0, waiting for transfers between devices: 867 us -> none  [the longest x8 682 us: image_every(): summed = lax.psum(local_terms(direction), 'ublk')]
    scatter-add x9 -> x0, other arithmetic: 237 us -> none  [the longest x8 210 us: local_terms(): jax.ops.segment_sum(along[:, None] * rows, items, num_segments=column_items)]
    pallas_call x0 -> x1, Pallas kernels: none -> 168 us  [body(): pl.pallas_call(kernel, name='als_cg', out_shape=(jax.ShapeDtypeStruct((OW...]
    gather x9 -> x0, local copies, waits for them, and re-layouts: 145 us -> none  [the longest x8 130 us: local_terms(): along = jnp.sum(rows * whole_dir[items], axis=1) * weight]
    all_gather x1 -> x0, waiting for transfers between devices: 33.5 us -> none  [body(): block = lax.all_gather(shard, 'salt', axis=0, tiled=True)]
    reduce_sum x15 -> x0, other arithmetic: 30.4 us -> none  [the longest x8 25.8 us: local_terms(): along = jnp.sum(rows * whole_dir[items], axis=1) * weight]
    dot_general x9 -> x0, matrix products: 14.8 us -> none  [the longest x8 13.8 us: finish(): jnp.dot(direction, gram, precision=lax.Precision.HIGHEST)]
  transfers between devices with their start and end apart: 11 -> 0, of which waited for: 11 -> 0; matrix products, arithmetic and copies ran while one was open for 4% -> 0% of each run, Pallas kernels for 0% -> 0%
where the time goes in v1:
time: 171 us
  Pallas kernels  168 us (98%)
  local copies, waits for them, and re-layouts  2 us (1%)
    pallas_call x1, Pallas kernels, body(): pl.pallas_call(kernel, name='als_cg', out_shape=(jax.ShapeDtypeStruct((OW...  168 us

profile of v1, /device:TPU:0, one launch (start us, length us, event | category | flops | bytes accessed | tf_op | source)
XLA Modules:
  0.0 171.2 jit_solution(12357456740841571494)
XLA Ops:
  1.3 167.9 %als_cg.1 = (f32[32,256]{1,0:T(8,128)}, f32[32,256]{1,0:T(8,128)}) custom-call(bf16[1024,256]{1,0:T(8,128)(2,1)} %bitcast.6, s32[1,4096]{1,0:T(1,128)} %bitcast.9, s32[1,4096]{1,0:T(1,128)} %bitcast.10, f32[1,4096]{1,0:T(1,128)} %bitcast.11, s32[1,1]{1,0:T(1,128)S(6)} %copy.9.live), custom_call_target="tpu_custom_call" | custom-call | tf_op jit(solution)/shard_map/als_cg/pallas_call | solution.py:293
  169.2 0.0 copy-start
  169.2 1.4 copy.10
  170.6 0.0 copy-done
  170.6 0.6 copy.11
Async XLA Ops:
  169.2 1.4 copy-start

commit v2 on v1

v2 whole, which is shorter than its diff:
```python
import jax
import jax.numpy as jnp
from jax import lax
from jax.experimental import pallas as pl
from jax.experimental.pallas import tpu as pltpu
from jax.sharding import PartitionSpec as P

ITERS = 8
REG = 1.0
EPS = 1e-06

X = 4
OWNERS = X * X
OWN = 32
RANK = 256
ITEMS = OWNERS * OWN
SLOTS = 4096
SHARD = 1024
SALT = 8
CHUNKS = 4
CHUNK = SHARD // CHUNKS
TILE = 1024
GRAM_OWN = RANK // OWNERS

F32 = jnp.float32
BF16 = jnp.bfloat16
MESH = pl.DeviceIdType.MESH


def ring(a):
    return min(a, X - a)


OFFSETS = sorted(
    [(dx, dz) for dx in range(X) for dz in range(X)],
    key=lambda o: (ring(o[0]) + ring(o[1]), o),
)
FAR_FIRST = list(range(OWNERS - 1, 0, -1))
GROUPS = 2
HALF = OWN // GROUPS
GROUP = OWNERS * HALF
UNIT = 512

PARTNER, UP, DOWN, ACROSS, P_UP, P_DOWN, P_ACROSS = range(7)


def kernel(
    shard, users, items, raw, live,
    x_out, r_out,
    block, weight, confid, rows_t, scaled_t, rows, mask, terms, gram, gram_sum, gram_in, gram_own,
    rhs, rhs_in, whole_dir, direction, own_terms, out_terms, in_terms,
    ag_send, ag_recv, gram_send, gram_recv, gall_send, gall_recv,
    rhs_send, rhs_recv, dir_send, dir_recv, loc_send, loc_recv,
):
    ublk = lax.axis_index("ublk")
    salt = lax.axis_index("salt")
    px, pz = lax.div(ublk, X), lax.rem(ublk, X)
    py, pc = lax.div(salt, 2), lax.rem(salt, 2)

    def owner(k, sign=1):
        dx, dz = OFFSETS[k]
        return lax.rem(px + sign * dx + X, X) * X + lax.rem(pz + sign * dz + X, X)

    def line(dy, core):
        return lax.rem(py + dy, X) * 2 + core

    def remote(src, dst, send, recv, device):
        copy = pltpu.make_async_remote_copy(
            src_ref=src, dst_ref=dst, send_sem=send, recv_sem=recv,
            device_id=device, device_id_type=MESH,
        )
        return copy

    barrier = pltpu.get_barrier_semaphore()
    peers = [(owner(k), salt) for k in range(1, OWNERS)]
    peers += [(ublk, line(1, pc)), (ublk, line(3, pc)), (ublk, line(0, 1 - pc))]
    for device in peers:
        pl.semaphore_signal(barrier, inc=1, device_id=device, device_id_type=MESH)

    for g in range(GROUPS):
        for k in range(OWNERS):
            place = items[...] - (owner(k) * OWN + g * HALF)
            chosen = place == lax.broadcasted_iota(jnp.int32, (HALF, SLOTS), 0)
            mask[pl.ds(g * GROUP + k * HALF, HALF)] = jnp.where(chosen, 1.0, 0.0).astype(BF16)
    alive = lax.broadcasted_iota(jnp.int32, (1, SLOTS), 1) < live[0, 0]
    weight[...] = jnp.where(alive, raw[...], 0.0)
    confid[...] = jnp.where(alive, 1.0 + raw[...], 0.0)

    def select(source, who, unit, first=False, last=None):
        part = source[pl.ds(unit * UNIT, UNIT)]
        part_t = part.T
        outer = jnp.dot(part_t, part, preferred_element_type=F32)
        if first:
            gram[...] = outer
        else:
            gram[...] += outer
        if last is not None:
            last()
        base = who * SHARD + unit * UNIT
        for n in range(SLOTS // TILE):
            at = pl.ds(n * TILE, TILE)
            chosen = (users[:, at] - base) == lax.broadcasted_iota(jnp.int32, (UNIT, TILE), 0)
            one_hot = jnp.where(chosen, 1.0, 0.0).astype(BF16)
            found = jnp.dot(part_t, one_hot, preferred_element_type=F32).astype(BF16)
            if not first:
                found = rows_t[:, at] + found
            if last is None:
                rows_t[:, at] = found
            else:
                rows[at] = found.T
                scaled_t[:, at] = (found.astype(F32) * weight[:, at]).astype(BF16)

    select(shard, salt, 0, first=True)
    pl.semaphore_wait(barrier, len(peers))

    def piece(ref, h):
        return ref.at[pl.ds(h * CHUNK, CHUNK)]

    def gathered(src, place, h, device):
        return remote(src, piece(block.at[place], h), ag_send.at[place, h], ag_recv.at[place, h], device)

    copies = {}
    for h in range(CHUNKS):
        copies[UP, h] = gathered(piece(shard, h), UP, h, (ublk, line(1, pc)))
        copies[DOWN, h] = gathered(piece(shard, h), DOWN, h, (ublk, line(3, pc)))
        copies[PARTNER, h] = gathered(piece(shard, h), PARTNER, h, (ublk, line(0, 1 - pc)))
        for place in (UP, DOWN, PARTNER):
            copies[place, h].start()

    def relay(h):
        for place in (UP, DOWN):
            copies[place, h].wait_recv()
        copies[ACROSS, h] = gathered(piece(block.at[UP + pc], h), ACROSS, h, (ublk, line(1 + 2 * pc, pc)))
        copies[P_UP, h] = gathered(piece(block.at[UP], h), P_UP, h, (ublk, line(0, 1 - pc)))
        copies[P_DOWN, h] = gathered(piece(block.at[DOWN], h), P_DOWN, h, (ublk, line(0, 1 - pc)))
        for place in (ACROSS, P_UP, P_DOWN):
            copies[place, h].start()

    def relay_across(h):
        copies[ACROSS, h].wait_recv()
        copies[P_ACROSS, h] = gathered(piece(block.at[ACROSS], h), P_ACROSS, h, (ublk, line(0, 1 - pc)))
        copies[P_ACROSS, h].start()

    whose = {
        PARTNER: line(0, 1 - pc), UP: line(3, pc), DOWN: line(1, pc), ACROSS: line(2, pc),
        P_UP: line(3, 1 - pc), P_DOWN: line(1, 1 - pc), P_ACROSS: line(2, 1 - pc),
    }

    def take(place, unit, last=None):
        if place in (PARTNER, P_UP, P_DOWN, P_ACROSS):
            for h in range(unit * UNIT // CHUNK, (unit + 1) * UNIT // CHUNK):
                copies[place, h].wait_recv()
        select(block.at[place], whose[place], unit, last=last)

    gram_copies = [
        remote(
            gram.at[pl.ds(pl.multiple_of(owner(k) * GRAM_OWN, GRAM_OWN), GRAM_OWN)], gram_in.at[k],
            gram_send.at[k], gram_recv.at[k], (owner(k), salt),
        )
        for k in range(OWNERS) if k
    ]

    def send_gram():
        for copy in reversed(gram_copies):
            copy.start()

    select(shard, salt, 1)
    take(PARTNER, 0)
    take(PARTNER, 1)
    relay(0)
    relay(1)
    take(UP, 0)
    relay(2)
    take(DOWN, 0)
    take(P_UP, 0)
    relay(3)
    take(P_DOWN, 0)
    take(UP, 1)
    relay_across(0)
    take(DOWN, 1)
    relay_across(1)
    take(P_UP, 1)
    relay_across(2)
    take(P_DOWN, 1)
    relay_across(3)
    take(ACROSS, 0)
    take(P_ACROSS, 0)
    take(ACROSS, 1)
    take(P_ACROSS, 1, last=send_gram)

    upper = confid[...].astype(BF16)
    lower = (confid[...] - upper.astype(F32)).astype(BF16)
    rhs_copies = {}
    for g in range(GROUPS):
        at = pl.ds(g * GROUP, GROUP)
        parts = []
        for level in (upper, lower):
            for n in range(SLOTS // TILE):
                cols = pl.ds(n * TILE, TILE)
                terms[at, cols] = jnp.where(
                    mask[at, cols] != 0, level[:, n * TILE:(n + 1) * TILE], jnp.zeros((), BF16)
                )
            parts.append(jnp.dot(terms[at], rows[...], preferred_element_type=F32))
        rhs[at] = parts[0] + parts[1]
        for k in FAR_FIRST:
            rhs_copies[g, k] = remote(
                rhs.at[pl.ds(g * GROUP + k * HALF, HALF)], rhs_in.at[g, k],
                rhs_send.at[g, k], rhs_recv.at[g, k], (owner(k), salt),
            )
            rhs_copies[g, k].start()

    own_rows = pl.ds(pl.multiple_of(ublk * GRAM_OWN, GRAM_OWN), GRAM_OWN)
    total = gram[own_rows]
    for k in range(1, OWNERS):
        gram_copies[k - 1].wait_recv()
        total = total + gram_in[k]
    gram_own[...] = total
    gram_sum[own_rows] = total
    gall_copies = [
        remote(
            gram_own, gram_sum.at[own_rows], gall_send.at[k], gall_recv.at[k], (owner(k), salt)
        )
        for k in range(OWNERS) if k
    ]

    dir_copies = {}
    loc_copies = {}
    for g in range(GROUPS):
        for k in range(1, OWNERS):
            dir_copies[g, k] = remote(
                whole_dir.at[pl.ds(g * GROUP, HALF)], whole_dir.at[pl.ds(g * GROUP + k * HALF, HALF)],
                dir_send.at[g, k], dir_recv.at[g, k], (owner(k, -1), salt),
            )
            loc_copies[g, k] = remote(
                out_terms.at[pl.ds(g * GROUP + k * HALF, HALF)], in_terms.at[g, k],
                loc_send.at[g, k], loc_recv.at[g, k], (owner(k), salt),
            )

    def send_direction(g, p):
        direction[pl.ds(g * HALF, HALF)] = p
        whole_dir[pl.ds(g * GROUP, HALF)] = p.astype(BF16)
        for k in FAR_FIRST:
            dir_copies[g, k].start()

    for g in range(GROUPS):
        own = pl.ds(g * HALF, HALF)
        total = rhs[pl.ds(g * GROUP, HALF)]
        for k in range(1, OWNERS):
            rhs_copies[g, k].wait_recv()
            total = total + rhs_in[g, k]
        send_direction(g, total)
        r_out[own] = total
        x_out[own] = jnp.zeros_like(total)
        if g == 0:
            for copy in reversed(gall_copies):
                copy.start()

    def iteration(t, carry):
        for g in range(GROUPS):
            at = pl.ds(g * GROUP, GROUP)
            for k in range(1, OWNERS):
                dir_copies[g, k].wait_recv()
            for n in range(SLOTS // TILE):
                cols = pl.ds(n * TILE, TILE)
                along = jnp.dot(whole_dir[at], scaled_t[:, cols], preferred_element_type=F32)
                terms[at, cols] = jnp.where(mask[at, cols] != 0, along.astype(BF16), jnp.zeros((), BF16))
            local = jnp.dot(terms[at], rows[...], preferred_element_type=F32)
            own_terms[pl.ds(g * HALF, HALF)] = local[:HALF]
            out_terms[at] = local.astype(BF16)
            for k in FAR_FIRST:
                loc_copies[g, k].start()

        @pl.when(t == 0)
        def _():
            for copy in gall_copies:
                copy.wait_recv()

        for g in range(GROUPS):
            own = pl.ds(g * HALF, HALF)
            p = direction[own]
            r = r_out[own]
            norm_now = jnp.sum(r * r, axis=1, keepdims=True)
            image = jnp.dot(p, gram_sum[...], precision=lax.Precision.HIGHEST, preferred_element_type=F32)
            image = image + REG * p + own_terms[own]
            for k in range(1, OWNERS):
                dir_copies[g, k].wait_send()
            for k in range(1, OWNERS):
                loc_copies[g, k].wait_recv()
                image = image + in_terms[g, k].astype(F32)
            alpha = norm_now / (jnp.sum(p * image, axis=1, keepdims=True) + EPS)
            x_out[own] += alpha * p
            r = r - alpha * image
            r_out[own] = r
            norm_next = jnp.sum(r * r, axis=1, keepdims=True)

            @pl.when(t < ITERS - 1)
            def _():
                send_direction(g, r + (norm_next / (norm_now + EPS)) * p)

            for k in range(1, OWNERS):
                loc_copies[g, k].wait_send()
        return carry

    lax.fori_loop(0, ITERS, iteration, 0)

    for copy in list(copies.values()) + gram_copies + gall_copies + list(rhs_copies.values()):
        copy.wait_send()


def body(user_factors, tile_users, tile_items, tile_weight, live_count):
    vmem = pl.BlockSpec(memory_space=pltpu.VMEM)
    dma = pltpu.SemaphoreType.DMA
    found, left = pl.pallas_call(
        kernel,
        name="als_cg",
        out_shape=(jax.ShapeDtypeStruct((OWN, RANK), F32), jax.ShapeDtypeStruct((OWN, RANK), F32)),
        in_specs=[vmem, vmem, vmem, vmem, pl.BlockSpec(memory_space=pltpu.SMEM)],
        out_specs=(vmem, vmem),
        scratch_shapes=[
            pltpu.VMEM((SALT - 1, SHARD, RANK), BF16),
            pltpu.VMEM((1, SLOTS), F32),
            pltpu.VMEM((1, SLOTS), F32),
            pltpu.VMEM((RANK, SLOTS), BF16),
            pltpu.VMEM((RANK, SLOTS), BF16),
            pltpu.VMEM((SLOTS, RANK), BF16),
            pltpu.VMEM((ITEMS, SLOTS), BF16),
            pltpu.VMEM((ITEMS, SLOTS), BF16),
            pltpu.VMEM((RANK, RANK), F32),
            pltpu.VMEM((RANK, RANK), F32),
            pltpu.VMEM((OWNERS, GRAM_OWN, RANK), F32),
            pltpu.VMEM((GRAM_OWN, RANK), F32),
            pltpu.VMEM((ITEMS, RANK), F32),
            pltpu.VMEM((GROUPS, OWNERS, HALF, RANK), F32),
            pltpu.VMEM((ITEMS, RANK), BF16),
            pltpu.VMEM((OWN, RANK), F32),
            pltpu.VMEM((OWN, RANK), F32),
            pltpu.VMEM((ITEMS, RANK), BF16),
            pltpu.VMEM((GROUPS, OWNERS, HALF, RANK), BF16),
            dma((SALT - 1, CHUNKS)), dma((SALT - 1, CHUNKS)),
            dma((OWNERS,)), dma((OWNERS,)), dma((OWNERS,)), dma((OWNERS,)),
            dma((GROUPS, OWNERS)), dma((GROUPS, OWNERS)), dma((GROUPS, OWNERS)), dma((GROUPS, OWNERS)),
            dma((GROUPS, OWNERS)), dma((GROUPS, OWNERS)),
        ],
        compiler_params=pltpu.CompilerParams(
            collective_id=0, has_side_effects=True, vmem_limit_bytes=56 * 2**20
        ),
    )(user_factors[0], tile_users[0], tile_items[0], tile_weight[0], live_count)
    return (found[None], left[None])


def solution(mesh):
    return jax.shard_map(
        body,
        mesh=mesh,
        in_specs=(
            P("ublk", "salt", None),
            P("ublk", "salt", None),
            P("ublk", "salt", None),
            P("ublk", "salt", None),
            P("ublk", "salt"),
        ),
        out_specs=(P("salt", "ublk", None), P("salt", "ublk", None)),
        check_vma=False,
    )
```

time: 171 us -> 149 us (0.87)
  Pallas kernels: 168 us -> 145 us
    pallas_call x1, Pallas kernels: 168 us -> 145 us  [body(): pl.pallas_call(kernel, name='als_cg', out_shape=(jax.ShapeDtypeStruct((OW...]
where the time goes in v2:
time: 149 us
  Pallas kernels  145 us (97%)
  local copies, waits for them, and re-layouts  2 us (1%)
    pallas_call x1, Pallas kernels, body(): pl.pallas_call(kernel, name='als_cg', out_shape=(jax.ShapeDtypeStruct((OW...  145 us

profile of v2, /device:TPU:0, one launch (start us, length us, event | category | flops | bytes accessed | tf_op | source)
XLA Modules:
  0.0 148.5 jit_solution(4591518736460702807)
XLA Ops:
  1.3 145.2 %als_cg.1 = (f32[32,256]{1,0:T(8,128)}, f32[32,256]{1,0:T(8,128)}) custom-call(bf16[1024,256]{1,0:T(8,128)(2,1)} %bitcast.6, s32[1,4096]{1,0:T(1,128)} %bitcast.9, s32[1,4096]{1,0:T(1,128)} %bitcast.10, f32[1,4096]{1,0:T(1,128)} %bitcast.11, s32[1,1]{1,0:T(1,128)S(6)} %copy.9.live), custom_call_target="tpu_custom_call" | custom-call | tf_op jit(solution)/shard_map/als_cg/pallas_call | solution.py:313
  146.5 0.0 copy-start
  146.5 1.4 copy.10
  147.9 0.0 copy-done
  147.9 0.6 copy.11
Async XLA Ops:
  146.5 1.4 copy-start

commit v3 on v2

--- a/solution.py
+++ b/solution.py
@@ -39,15 +39,16 @@
 GROUPS = 2
 HALF = OWN // GROUPS
 GROUP = OWNERS * HALF
+PARTS = (range(0, OWNERS // 2), range(OWNERS // 2, OWNERS))
 UNIT = 512
 
 PARTNER, UP, DOWN, ACROSS, P_UP, P_DOWN, P_ACROSS = range(7)
 
 
 def kernel(
-    shard, users, items, raw, live,
+    shard_in, users_in, items_in, raw_in, live,
     x_out, r_out,
-    block, weight, confid, rows_t, scaled_t, rows, mask, terms, gram, gram_sum, gram_in, gram_own,
+    shard, users, items, raw, load_sem, block, weight, confid, rows_t, scaled_t, rows, mask, terms, gram, gram_sum, gram_in, gram_own,
     rhs, rhs_in, whole_dir, direction, own_terms, out_terms, in_terms,
     ag_send, ag_recv, gram_send, gram_recv, gall_send, gall_recv,
     rhs_send, rhs_recv, dir_send, dir_recv, loc_send, loc_recv,
@@ -65,11 +66,10 @@
         return lax.rem(py + dy, X) * 2 + core
 
     def remote(src, dst, send, recv, device):
-        copy = pltpu.make_async_remote_copy(
+        return pltpu.make_async_remote_copy(
             src_ref=src, dst_ref=dst, send_sem=send, recv_sem=recv,
             device_id=device, device_id_type=MESH,
         )
-        return copy
 
     barrier = pltpu.get_barrier_semaphore()
     peers = [(owner(k), salt) for k in range(1, OWNERS)]
@@ -77,17 +77,8 @@
     for device in peers:
         pl.semaphore_signal(barrier, inc=1, device_id=device, device_id_type=MESH)
 
-    for g in range(GROUPS):
-        for k in range(OWNERS):
-            place = items[...] - (owner(k) * OWN + g * HALF)
-            chosen = place == lax.broadcasted_iota(jnp.int32, (HALF, SLOTS), 0)
-            mask[pl.ds(g * GROUP + k * HALF, HALF)] = jnp.where(chosen, 1.0, 0.0).astype(BF16)
-    alive = lax.broadcasted_iota(jnp.int32, (1, SLOTS), 1) < live[0, 0]
-    weight[...] = jnp.where(alive, raw[...], 0.0)
-    confid[...] = jnp.where(alive, 1.0 + raw[...], 0.0)
-
-    def select(source, who, unit, first=False, last=None):
-        part = source[pl.ds(unit * UNIT, UNIT)]
+    def select(source, who, start, size, first=False, last=None):
+        part = source[pl.ds(start, size)]
         part_t = part.T
         outer = jnp.dot(part_t, part, preferred_element_type=F32)
         if first:
@@ -96,10 +87,10 @@
             gram[...] += outer
         if last is not None:
             last()
-        base = who * SHARD + unit * UNIT
+        base = who * SHARD + start
         for n in range(SLOTS // TILE):
             at = pl.ds(n * TILE, TILE)
-            chosen = (users[:, at] - base) == lax.broadcasted_iota(jnp.int32, (UNIT, TILE), 0)
+            chosen = (users[:, at] - base) == lax.broadcasted_iota(jnp.int32, (size, TILE), 0)
             one_hot = jnp.where(chosen, 1.0, 0.0).astype(BF16)
             found = jnp.dot(part_t, one_hot, preferred_element_type=F32).astype(BF16)
             if not first:
@@ -110,47 +101,48 @@
                 rows[at] = found.T
                 scaled_t[:, at] = (found.astype(F32) * weight[:, at]).astype(BF16)
 
-    select(shard, salt, 0, first=True)
+    loads = [
+        pltpu.make_async_copy(source, target, load_sem.at[n])
+        for n, (source, target) in enumerate(
+            ((shard_in, shard), (users_in, users), (items_in, items), (raw_in, raw))
+        )
+    ]
+    for copy in loads:
+        copy.start()
+    for copy in loads:
+        copy.wait()
     pl.semaphore_wait(barrier, len(peers))
 
-    def piece(ref, h):
-        return ref.at[pl.ds(h * CHUNK, CHUNK)]
-
-    def gathered(src, place, h, device):
-        return remote(src, piece(block.at[place], h), ag_send.at[place, h], ag_recv.at[place, h], device)
-
-    copies = {}
-    for h in range(CHUNKS):
-        copies[UP, h] = gathered(piece(shard, h), UP, h, (ublk, line(1, pc)))
-        copies[DOWN, h] = gathered(piece(shard, h), DOWN, h, (ublk, line(3, pc)))
-        copies[PARTNER, h] = gathered(piece(shard, h), PARTNER, h, (ublk, line(0, 1 - pc)))
-        for place in (UP, DOWN, PARTNER):
-            copies[place, h].start()
-
-    def relay(h):
-        for place in (UP, DOWN):
-            copies[place, h].wait_recv()
-        copies[ACROSS, h] = gathered(piece(block.at[UP + pc], h), ACROSS, h, (ublk, line(1 + 2 * pc, pc)))
-        copies[P_UP, h] = gathered(piece(block.at[UP], h), P_UP, h, (ublk, line(0, 1 - pc)))
-        copies[P_DOWN, h] = gathered(piece(block.at[DOWN], h), P_DOWN, h, (ublk, line(0, 1 - pc)))
-        for place in (ACROSS, P_UP, P_DOWN):
-            copies[place, h].start()
-
-    def relay_across(h):
-        copies[ACROSS, h].wait_recv()
-        copies[P_ACROSS, h] = gathered(piece(block.at[ACROSS], h), P_ACROSS, h, (ublk, line(0, 1 - pc)))
-        copies[P_ACROSS, h].start()
+    partner = (ublk, line(0, 1 - pc))
+
+    def moved(place, h):
+        start = h * CHUNK if isinstance(h, int) else pl.multiple_of(h * CHUNK, CHUNK)
+        piece = pl.ds(start, CHUNK)
+        source, device = {
+            UP: (shard, (ublk, line(1, pc))),
+            DOWN: (shard, (ublk, line(3, pc))),
+            PARTNER: (shard, partner),
+            ACROSS: (block.at[UP + pc], (ublk, line(1 + 2 * pc, pc))),
+            P_UP: (block.at[UP], partner),
+            P_DOWN: (block.at[DOWN], partner),
+            P_ACROSS: (block.at[ACROSS], partner),
+        }[place]
+        return remote(
+            source.at[piece], block.at[place, piece], ag_send.at[place, h], ag_recv.at[place, h], device
+        )
 
     whose = {
         PARTNER: line(0, 1 - pc), UP: line(3, pc), DOWN: line(1, pc), ACROSS: line(2, pc),
         P_UP: line(3, 1 - pc), P_DOWN: line(1, 1 - pc), P_ACROSS: line(2, 1 - pc),
     }
 
-    def take(place, unit, last=None):
-        if place in (PARTNER, P_UP, P_DOWN, P_ACROSS):
-            for h in range(unit * UNIT // CHUNK, (unit + 1) * UNIT // CHUNK):
-                copies[place, h].wait_recv()
-        select(block.at[place], whose[place], unit, last=last)
+    def take(place, h, last=None):
+        start = h * CHUNK if isinstance(h, int) else pl.multiple_of(h * CHUNK, CHUNK)
+        select(block.at[place], whose[place], start, CHUNK, last=last)
+
+    for h in range(CHUNKS):
+        for place in (UP, DOWN, PARTNER):
+            moved(place, h).start()
 
     gram_copies = [
         remote(
@@ -164,29 +156,53 @@
         for copy in reversed(gram_copies):
             copy.start()
 
-    select(shard, salt, 1)
-    take(PARTNER, 0)
-    take(PARTNER, 1)
-    relay(0)
-    relay(1)
-    take(UP, 0)
-    relay(2)
-    take(DOWN, 0)
-    take(P_UP, 0)
-    relay(3)
-    take(P_DOWN, 0)
-    take(UP, 1)
-    relay_across(0)
-    take(DOWN, 1)
-    relay_across(1)
-    take(P_UP, 1)
-    relay_across(2)
-    take(P_DOWN, 1)
-    relay_across(3)
-    take(ACROSS, 0)
-    take(P_ACROSS, 0)
-    take(ACROSS, 1)
-    take(P_ACROSS, 1, last=send_gram)
+    select(shard, salt, 0, UNIT, first=True)
+    select(shard, salt, UNIT, UNIT)
+
+    for g in range(GROUPS):
+        for k in range(OWNERS):
+            place = items[...] - (owner(k) * OWN + g * HALF)
+            chosen = place == lax.broadcasted_iota(jnp.int32, (HALF, SLOTS), 0)
+            mask[pl.ds(g * GROUP + k * HALF, HALF)] = jnp.where(chosen, 1.0, 0.0).astype(BF16)
+    alive = lax.broadcasted_iota(jnp.int32, (1, SLOTS), 1) < live[0, 0]
+    weight[...] = jnp.where(alive, raw[...], 0.0)
+    confid[...] = jnp.where(alive, 1.0 + raw[...], 0.0)
+
+    for unit in range(SHARD // UNIT):
+        for h in range(unit * UNIT // CHUNK, (unit + 1) * UNIT // CHUNK):
+            moved(PARTNER, h).wait_recv()
+        select(block.at[PARTNER], whose[PARTNER], unit * UNIT, UNIT)
+
+    def near(h, carry):
+        for place in (UP, DOWN):
+            moved(place, h).wait_recv()
+        for place in (P_UP, P_DOWN, ACROSS):
+            moved(place, h).start()
+        take(UP, h)
+        take(DOWN, h)
+        for place in (P_UP, P_DOWN):
+            moved(place, h).wait_recv()
+            take(place, h)
+        return carry
+
+    lax.fori_loop(0, CHUNKS, near, 0)
+
+    def hand_over(h):
+        moved(ACROSS, h).wait_recv()
+        moved(P_ACROSS, h).start()
+
+    def far(h, carry):
+        take(ACROSS, h)
+        hand_over(h + 1)
+        moved(P_ACROSS, h).wait_recv()
+        take(P_ACROSS, h)
+        return carry
+
+    hand_over(0)
+    lax.fori_loop(0, CHUNKS - 1, far, 0)
+    take(ACROSS, CHUNKS - 1)
+    moved(P_ACROSS, CHUNKS - 1).wait_recv()
+    take(P_ACROSS, CHUNKS - 1, last=send_gram)
 
     upper = confid[...].astype(BF16)
     lower = (confid[...] - upper.astype(F32)).astype(BF16)
@@ -229,12 +245,25 @@
         for k in range(1, OWNERS):
             dir_copies[g, k] = remote(
                 whole_dir.at[pl.ds(g * GROUP, HALF)], whole_dir.at[pl.ds(g * GROUP + k * HALF, HALF)],
-                dir_send.at[g, k], dir_recv.at[g, k], (owner(k, -1), salt),
+                dir_send.at[g], dir_recv.at[g, k // (OWNERS // 2)], (owner(k, -1), salt),
             )
             loc_copies[g, k] = remote(
                 out_terms.at[pl.ds(g * GROUP + k * HALF, HALF)], in_terms.at[g, k],
-                loc_send.at[g, k], loc_recv.at[g, k], (owner(k), salt),
+                loc_send.at[g], loc_recv.at[g], (owner(k), salt),
             )
+
+    dir_waits = {}
+    dir_all = {}
+    loc_all = {}
+    for g in range(GROUPS):
+        for part, places in enumerate(PARTS):
+            first = max(places[0], 1)
+            rest = whole_dir.at[pl.ds(g * GROUP + first * HALF, (places[-1] + 1 - first) * HALF)]
+            dir_waits[g, places[0]] = remote(rest, rest, dir_send.at[g], dir_recv.at[g, part], partner)
+        rest = whole_dir.at[pl.ds(g * GROUP + HALF, GROUP - HALF)]
+        dir_all[g] = remote(rest, rest, dir_send.at[g], dir_recv.at[g, 0], partner)
+        others = in_terms.at[g, pl.ds(1, OWNERS - 1)]
+        loc_all[g] = remote(others, others, loc_send.at[g], loc_recv.at[g], partner)
 
     def send_direction(g, p):
         direction[pl.ds(g * HALF, HALF)] = p
@@ -257,18 +286,20 @@
 
     def iteration(t, carry):
         for g in range(GROUPS):
-            at = pl.ds(g * GROUP, GROUP)
-            for k in range(1, OWNERS):
-                dir_copies[g, k].wait_recv()
-            for n in range(SLOTS // TILE):
-                cols = pl.ds(n * TILE, TILE)
-                along = jnp.dot(whole_dir[at], scaled_t[:, cols], preferred_element_type=F32)
-                terms[at, cols] = jnp.where(mask[at, cols] != 0, along.astype(BF16), jnp.zeros((), BF16))
-            local = jnp.dot(terms[at], rows[...], preferred_element_type=F32)
-            own_terms[pl.ds(g * HALF, HALF)] = local[:HALF]
-            out_terms[at] = local.astype(BF16)
-            for k in FAR_FIRST:
-                loc_copies[g, k].start()
+            for sub in PARTS:
+                at = pl.ds(g * GROUP + sub[0] * HALF, len(sub) * HALF)
+                dir_waits[g, sub[0]].wait_recv()
+                for n in range(SLOTS // TILE):
+                    cols = pl.ds(n * TILE, TILE)
+                    along = jnp.dot(whole_dir[at], scaled_t[:, cols], preferred_element_type=F32)
+                    terms[at, cols] = jnp.where(mask[at, cols] != 0, along.astype(BF16), jnp.zeros((), BF16))
+                local = jnp.dot(terms[at], rows[...], preferred_element_type=F32)
+                if sub[0] == 0:
+                    own_terms[pl.ds(g * HALF, HALF)] = local[:HALF]
+                out_terms[at] = local.astype(BF16)
+                for k in reversed(sub):
+                    if k:
+                        loc_copies[g, k].start()
 
         @pl.when(t == 0)
         def _():
@@ -282,10 +313,9 @@
             norm_now = jnp.sum(r * r, axis=1, keepdims=True)
             image = jnp.dot(p, gram_sum[...], precision=lax.Precision.HIGHEST, preferred_element_type=F32)
             image = image + REG * p + own_terms[own]
+            dir_all[g].wait_send()
+            loc_all[g].wait_recv()
             for k in range(1, OWNERS):
-                dir_copies[g, k].wait_send()
-            for k in range(1, OWNERS):
-                loc_copies[g, k].wait_recv()
                 image = image + in_terms[g, k].astype(F32)
             alpha = norm_now / (jnp.sum(p * image, axis=1, keepdims=True) + EPS)
             x_out[own] += alpha * p
@@ -297,13 +327,15 @@
             def _():
                 send_direction(g, r + (norm_next / (norm_now + EPS)) * p)
 
-            for k in range(1, OWNERS):
-                loc_copies[g, k].wait_send()
+            loc_all[g].wait_send()
         return carry
 
     lax.fori_loop(0, ITERS, iteration, 0)
 
-    for copy in list(copies.values()) + gram_copies + gall_copies + list(rhs_copies.values()):
+    for place in range(SALT - 1):
+        for h in range(CHUNKS):
+            moved(place, h).wait_send()
+    for copy in gram_copies + gall_copies + list(rhs_copies.values()):
         copy.wait_send()
 
 
@@ -314,9 +346,14 @@
         kernel,
         name="als_cg",
         out_shape=(jax.ShapeDtypeStruct((OWN, RANK), F32), jax.ShapeDtypeStruct((OWN, RANK), F32)),
-        in_specs=[vmem, vmem, vmem, vmem, pl.BlockSpec(memory_space=pltpu.SMEM)],
+        in_specs=[pl.BlockSpec(memory_space=pl.ANY)] * 4 + [pl.BlockSpec(memory_space=pltpu.SMEM)],
         out_specs=(vmem, vmem),
         scratch_shapes=[
+            pltpu.VMEM((SHARD, RANK), BF16),
+            pltpu.VMEM((1, SLOTS), jnp.int32),
+            pltpu.VMEM((1, SLOTS), jnp.int32),
+            pltpu.VMEM((1, SLOTS), F32),
+            dma((4,)),
             pltpu.VMEM((SALT - 1, SHARD, RANK), BF16),
             pltpu.VMEM((1, SLOTS), F32),
             pltpu.VMEM((1, SLOTS), F32),
@@ -338,8 +375,8 @@
             pltpu.VMEM((GROUPS, OWNERS, HALF, RANK), BF16),
             dma((SALT - 1, CHUNKS)), dma((SALT - 1, CHUNKS)),
             dma((OWNERS,)), dma((OWNERS,)), dma((OWNERS,)), dma((OWNERS,)),
-            dma((GROUPS, OWNERS)), dma((GROUPS, OWNERS)), dma((GROUPS, OWNERS)), dma((GROUPS, OWNERS)),
             dma((GROUPS, OWNERS)), dma((GROUPS, OWNERS)),
+            dma((GROUPS,)), dma((GROUPS, len(PARTS))), dma((GROUPS,)), dma((GROUPS,)),
         ],
         compiler_params=pltpu.CompilerParams(
             collective_id=0, has_side_effects=True, vmem_limit_bytes=56 * 2**20

time: 149 us -> 144 us (0.966)
  Pallas kernels: 145 us -> 140 us
    pallas_call x1, Pallas kernels: 145 us -> 140 us  [body(): pl.pallas_call(kernel, name='als_cg', out_shape=(jax.ShapeDtypeStruct((OW...]
where the time goes in v3:
time: 144 us
  Pallas kernels  140 us (97%)
  local copies, waits for them, and re-layouts  2 us (1%)
    pallas_call x1, Pallas kernels, body(): pl.pallas_call(kernel, name='als_cg', out_shape=(jax.ShapeDtypeStruct((OW...  140 us

profile of v3, /device:TPU:0, one launch (start us, length us, event | category | flops | bytes accessed | tf_op | source)
XLA Modules:
  0.0 143.7 jit_solution(15871559105427349503)
XLA Ops:
  1.3 140.4 %als_cg.1 = (f32[32,256]{1,0:T(8,128)}, f32[32,256]{1,0:T(8,128)}) custom-call(bf16[1024,256]{1,0:T(8,128)(2,1)} %bitcast.6, s32[1,4096]{1,0:T(1,128)} %bitcast.9, s32[1,4096]{1,0:T(1,128)} %bitcast.10, f32[1,4096]{1,0:T(1,128)} %bitcast.11, s32[1,1]{1,0:T(1,128)S(6)} %copy.9.live), custom_call_target="tpu_custom_call" | custom-call | tf_op jit(solution)/shard_map/als_cg/pallas_call | solution.py:345
  141.7 0.0 copy-start
  141.7 1.4 copy.10
  143.1 0.0 copy-done
  143.1 0.6 copy.11
Async XLA Ops:
  141.7 1.4 copy-start

commit v4 on v3

--- a/solution.py
+++ b/solution.py
@@ -47,12 +47,13 @@
 
 def kernel(
     shard_in, users_in, items_in, raw_in, live,
-    x_out, r_out,
+    both_out,
     shard, users, items, raw, load_sem, block, weight, confid, rows_t, scaled_t, rows, mask, terms, gram, gram_sum, gram_in, gram_own,
     rhs, rhs_in, whole_dir, direction, own_terms, out_terms, in_terms,
     ag_send, ag_recv, gram_send, gram_recv, gall_send, gall_recv,
     rhs_send, rhs_recv, dir_send, dir_recv, loc_send, loc_recv,
 ):
+    x_out, r_out = both_out.at[0], both_out.at[1]
     ublk = lax.axis_index("ublk")
     salt = lax.axis_index("salt")
     px, pz = lax.div(ublk, X), lax.rem(ublk, X)
@@ -280,9 +281,9 @@
         send_direction(g, total)
         r_out[own] = total
         x_out[own] = jnp.zeros_like(total)
-        if g == 0:
-            for copy in reversed(gall_copies):
-                copy.start()
+
+    for copy in reversed(gall_copies):
+        copy.start()
 
     def iteration(t, carry):
         for g in range(GROUPS):
@@ -342,12 +343,12 @@
 def body(user_factors, tile_users, tile_items, tile_weight, live_count):
     vmem = pl.BlockSpec(memory_space=pltpu.VMEM)
     dma = pltpu.SemaphoreType.DMA
-    found, left = pl.pallas_call(
+    both = pl.pallas_call(
         kernel,
         name="als_cg",
-        out_shape=(jax.ShapeDtypeStruct((OWN, RANK), F32), jax.ShapeDtypeStruct((OWN, RANK), F32)),
+        out_shape=jax.ShapeDtypeStruct((2, OWN, RANK), F32),
         in_specs=[pl.BlockSpec(memory_space=pl.ANY)] * 4 + [pl.BlockSpec(memory_space=pltpu.SMEM)],
-        out_specs=(vmem, vmem),
+        out_specs=vmem,
         scratch_shapes=[
             pltpu.VMEM((SHARD, RANK), BF16),
             pltpu.VMEM((1, SLOTS), jnp.int32),
@@ -382,7 +383,7 @@
             collective_id=0, has_side_effects=True, vmem_limit_bytes=56 * 2**20
         ),
     )(user_factors[0], tile_users[0], tile_items[0], tile_weight[0], live_count)
-    return (found[None], left[None])
+    return (both[:1], both[1:])
 
 
 def solution(mesh):

time: 144 us -> 142 us (0.986)
    unnamed x4 -> x0, local copies, waits for them, and re-layouts: 2 us -> none
where the time goes in v4:
time: 142 us
  Pallas kernels  139 us (98%)
    pallas_call x1, Pallas kernels, body(): pl.pallas_call(kernel, name='als_cg', out_shape=jax.ShapeDtypeStruct((2,...  139 us

profile of v4, /device:TPU:0, one launch (start us, length us, event | category | flops | bytes accessed | tf_op | source)
XLA Modules:
  0.0 142.1 jit_solution(9953717710450663814)
XLA Ops:
  1.3 139.4 %als_cg.1 = f32[2,32,256]{2,1,0:T(8,128)} custom-call(bf16[1024,256]{1,0:T(8,128)(2,1)} %bitcast.4, s32[1,4096]{1,0:T(1,128)} %bitcast.5, s32[1,4096]{1,0:T(1,128)} %bitcast.6, f32[1,4096]{1,0:T(1,128)} %bitcast.7, s32[1,1]{1,0:T(1,128)S(6)} %copy.7.live), custom_call_target="tpu_custom_call" | custom-call | tf_op jit(solution)/shard_map/als_cg/pallas_call | solution.py:346
  140.7 1.4 fusion

commit v5 on v4

--- a/solution.py
+++ b/solution.py
@@ -177,7 +177,7 @@
     def near(h, carry):
         for place in (UP, DOWN):
             moved(place, h).wait_recv()
-        for place in (P_UP, P_DOWN, ACROSS):
+        for place in (ACROSS, P_UP, P_DOWN):
             moved(place, h).start()
         take(UP, h)
         take(DOWN, h)

time: 142 us -> 143 us (level)
  no operation moved by 1% of the time
where the time goes in v5:
time: 143 us
  Pallas kernels  140 us (98%)
    pallas_call x1, Pallas kernels, body(): pl.pallas_call(kernel, name='als_cg', out_shape=jax.ShapeDtypeStruct((2,...  140 us

profile of v5, /device:TPU:0, one launch (start us, length us, event | category | flops | bytes accessed | tf_op | source)
XLA Modules:
  0.0 142.6 jit_solution(16159063918558349300)
XLA Ops:
  1.3 140.0 %als_cg.1 = f32[2,32,256]{2,1,0:T(8,128)} custom-call(bf16[1024,256]{1,0:T(8,128)(2,1)} %bitcast.4, s32[1,4096]{1,0:T(1,128)} %bitcast.5, s32[1,4096]{1,0:T(1,128)} %bitcast.6, f32[1,4096]{1,0:T(1,128)} %bitcast.7, s32[1,1]{1,0:T(1,128)S(6)} %copy.7.live), custom_call_target="tpu_custom_call" | custom-call | tf_op jit(solution)/shard_map/als_cg/pallas_call | solution.py:346
  141.2 1.4 fusion
